TPU v7x, 256 devices: a whole 4x4x8 slice. The times are simulated.
256 devices in a mesh: seq: 32 (over x, z), head: 8 (over y, core).
Axes of the slice: x: 4, y: 4, z: 8, core: 2. Of those that a mesh axis runs over, the one named last changes fastest.
Arguments:
- cached_probs: bfloat16 [128, 40, 8, 128, 128], P('seq', 'head'), may hold values from 0 to 1, as said below
- out_old: bfloat16 [16384, 5120], P('seq', 'head'), may hold values from -6 to 6
- key_lists: int32 [128, 8], P('seq'), may hold values from 0 to 127, as said below
- changed_block_numbers: int32 [32], replicated, may hold values from 0 to 127, as said below
- delta_v: bfloat16 [4096, 1024], P('seq', 'head'), may hold values from -24 to 24
- w_out: bfloat16 [5120, 5120], P('head', 'seq'), may hold values from -0.078125 to 0.078125
Outputs:
- attn_new: bfloat16 [16384, 5120], P('seq', 'head')
- out_proj: bfloat16 [16384, 5120], P('seq', 'head')
Inputs may be any that keep to these rules, and one draw needn't show every extreme that they name: `changed_block_numbers`: the changed block numbers are all different; the first block and the last block are always among them. `key_lists`: each query block lists 8 different key blocks; some list many changed blocks, most list few. `cached_probs`: for each query block, head and row, the weights over the row's listed keys are positive and sum to at most 1.
All inputs are finite; a program needn't handle non-finite values.
Results may differ from a plain program's by a relative error of at most 0.017.
Values may be sent and summed in bfloat16 or wider, within the bound.
A program may use at most 128 MiB of HBM per device.

v0:
```python
import jax
import jax.numpy as jnp
from jax import lax
from jax.sharding import PartitionSpec as P

HD = 128
BLK = 128
GROUP = 5


def local(cached_probs, out_old, key_lists, changed_block_numbers, delta_v, w_out):
    blocks_here = cached_probs.shape[0]
    heads_here = cached_probs.shape[1]
    topk_here = cached_probs.shape[2]
    values_here = heads_here // GROUP
    change_rows = delta_v.reshape(delta_v.shape[0] // BLK, BLK * values_here * HD)
    flat_lists = key_lists.reshape(blocks_here * topk_here)
    every_change = lax.all_gather(change_rows, "seq", axis=0, tiled=True)
    onehot = (flat_lists[:, None] == changed_block_numbers[None, :]).astype(jnp.bfloat16)
    selected = jnp.dot(onehot, every_change, preferred_element_type=jnp.float32)
    picked = selected.astype(jnp.bfloat16).reshape(blocks_here, topk_here, BLK, values_here, HD)
    tiles = cached_probs.reshape(blocks_here, values_here, GROUP, topk_here, BLK, BLK)
    delta_out = jnp.einsum("qvgkij,qkjvd->qivgd", tiles, picked, preferred_element_type=jnp.float32)
    delta_out = delta_out.reshape(blocks_here * BLK, heads_here * HD)
    attn_new = (out_old.astype(jnp.float32) + delta_out).astype(jnp.bfloat16)
    terms = jnp.dot(
        attn_new,
        lax.all_gather(w_out, "seq", axis=1, tiled=True),
        preferred_element_type=jnp.float32,
    )
    out_proj = lax.psum_scatter(terms.astype(jnp.bfloat16), "head", scatter_dimension=1, tiled=True)
    return (attn_new, out_proj)


def solution(mesh):
    placed = (
        P("seq", "head", None, None, None),
        P("seq", "head"),
        P("seq", None),
        P(),
        P("seq", "head"),
        P("head", "seq"),
    )
    return jax.shard_map(
        local,
        mesh=mesh,
        in_specs=placed,
        out_specs=(P("seq", "head"), P("seq", "head")),
        check_vma=False,
    )
```

profile of v0, /device:TPU:2, one launch (start us, length us, event | category | flops | bytes accessed | tf_op | source)
XLA Modules:
  0.0 247.0 jit_solution(4615410390081621917)
XLA Ops:
  7.2 0.0 all-gather.6.cloned.1.call-start
  7.2 1.4 reshape.24
  8.6 0.0 all-gather.6.cloned.1.call-update
  8.6 0.0 all-gather.4.cloned.1.call-start
  8.7 0.7 all-gather.4.cloned.1.call-update
  9.4 0.0 copy-start.1
  9.4 0.0 copy-start
  9.4 0.0 copy-start.2
  9.4 0.0 reduce-scatter.4.cloned.1.call-start
  9.5 8.7 %copy.14 = bf16[4,5,8,128,128]{3,2,4,1,0:T(8,128)(2,1)} copy(bf16[4,5,8,128,128]{4,3,2,1,0:T(8,128)(2,1)} %param.6) | data formatting | bytes 10485760 | tf_op args[0]
  18.1 0.0 copy-done.1
  18.1 0.1 eq.15
  18.2 0.0 copy-done
  18.2 0.3 copy.13
  18.5 72.4 %all-gather.6.cloned.1.call-done = bf16[32,1,16384]{2,1,0:T(2,128)(2,1)} async-done(((bf16[1,1,16384]{2,1,0:T(2,128)(2,1)}), bf16[32,1,16384]{2,1,0:T(2,128)(2,1)}) %all-gather.6.cloned.1.call-update) | async-done | bytes 1048592 | tf_op jit(solution)/shard_map/all_gather | solution.py:18
  90.9 0.0 copy-done.2
  90.9 5.3 %convolution_bitcast_fusion = f32[4,128,1,5,128]{1,4,3,0,2:T(8,128)S(1)} fusion(bf16[4,5,8,128,128]{3,2,4,1,0:T(8,128)(2,1)} %copy.14, bf16[32,1,16384]{2,1,0:T(2,128)(2,1)} %all-gather.6.cloned.1.call-done, s32[32]{0:T(128)S(1)} %copy-done.2, s32[32]{0:T(128)S(1)} %eq.15), kind=kOutput, calls=%fused_computation.2 | convolution fusion | flops 705168384 | bytes 7602432 | tf_op jit(solution)/shard_map/qvgkij,qkjvd->qivgd/dot_general | solution.py:23
  96.2 0.8 copy.15
  97.1 0.3 fusion.1
  97.3 83.0 %all-gather.4.cloned.1.call-done = bf16[640,5120]{0,1:T(8,128)(2,1)} async-done(((bf16[640,160]{0,1:T(8,128)(2,1)}), bf16[640,5120]{0,1:T(8,128)(2,1)}) %all-gather.4.cloned.1.call-update) | async-done | bytes 6553616 | tf_op jit(solution)/shard_map/all_gather | solution.py:28
  180.3 8.9 %convolution_convert_fusion.1 = bf16[512,5120]{1,0:T(8,128)(2,1)} fusion(bf16[512,640]{0,1:T(8,128)(2,1)S(1)} %fusion.1, bf16[640,5120]{0,1:T(8,128)(2,1)} %all-gather.4.cloned.1.call-done), kind=kOutput, calls=%fused_computation.1 | convolution fusion | flops 3358064640 | bytes 12451840 | tf_op jit(solution)/shard_map/dot_general | solution.py:26
  189.3 7.9 %copy.19 = bf16[512,5120]{0,1:T(8,128)(2,1)} copy(bf16[512,5120]{1,0:T(8,128)(2,1)} %convolution_convert_fusion.1) | data formatting | bytes 10485760
  197.2 0.0 reduce-scatter.4.cloned.1.call-update
  197.2 1.1 copy.16
  198.3 40.0 %reduce-scatter.4.cloned.1.call-done = bf16[640,512]{1,0:T(8,128)(2,1)} async-done(((bf16[5120,512]{1,0:T(8,128)(2,1)}), bf16[640,512]{1,0:T(8,128)(2,1)}) %reduce-scatter.4.cloned.1.call-update) | async-done | bytes 655376
  238.3 2.2 copy.20
Async XLA Ops:
  7.2 83.7 %all-gather.6.cloned.1.call-start = ((), (), s32[]{:S(2)}) async-start(), calls=%async_computation.2 | async-start | bytes 2162688 | tf_op jit(solution)/shard_map/all_gather | solution.py:18
  8.6 171.7 %all-gather.4.cloned.1.call-start = ((), (), s32[]{:S(2)}) async-start(), calls=%async_computation.1 | async-start | bytes 6758400 | tf_op jit(solution)/shard_map/all_gather | solution.py:28
  9.4 8.7 %copy-start.1 = (s32[4,8]{1,0:T(4,128)S(1)}, s32[4,8]{1,0:T(4,128)}, u32[]{:S(2)}) copy-start(s32[4,8]{1,0:T(4,128)} %param.8) | copy-start | bytes 388
  9.4 8.8 %copy-start = (bf16[512,640]{1,0:T(8,128)(2,1)S(1)}, bf16[512,640]{1,0:T(8,128)(2,1)}, u32[]{:S(2)}) copy-start(bf16[512,640]{1,0:T(8,128)(2,1)} %param.7) | copy-start | bytes 1966084
  9.4 81.5 %copy-start.2 = (s32[32]{0:T(128)S(1)}, s32[32]{0:T(128)}, u32[]{:S(2)}) copy-start(s32[32]{0:T(128)} %param.9) | copy-start | bytes 388
  9.4 228.8 %reduce-scatter.4.cloned.1.call-start = ((), (), s32[]{:S(2)}) async-start(), calls=%async_computation.3 | async-start | bytes 5898240
Sparse Core Ops, SparseCore 0:
  11.2 79.6 all-gather.5
  93.5 86.8 all-gather.3
  197.3 40.8 reduce-scatter.3
where the time goes:
time: 248 us; the launch traced here: 247 us
  waiting for transfers between devices  196 us (79%)
  local copies, waits for them, and re-layouts  22.4 us (9%)
  matrix products  14.3 us (6%)
  between operations  13.8 us (6%)
    all_gather x1, waiting for transfers between devices, local(): lax.all_gather(w_out, 'seq', axis=1, tiled=True)  83 us
    all_gather x1, waiting for transfers between devices, local(): every_change = lax.all_gather(change_rows, 'seq', axis=0, tiled=True)  72.4 us
    unnamed x4, waiting for transfers between devices  40.7 us
    unnamed x12, local copies, waits for them, and re-layouts  21.5 us
    dot_general x1, matrix products, local(): jnp.dot(attn_new, lax.all_gather(w_out, 'seq', axis=1, tiled=True), prefe...  8.95 us
    dot_general x1, matrix products, local(): jnp.einsum('qvgkij,qkjvd->qivgd', tiles, picked, preferred_element_type=j...  5.33 us
  transfers between devices with their start and end apart: 3, of which 3 were waited for; matrix products, arithmetic and copies ran while one was open for 7% of the time, Pallas kernels for 0%

commit v1 on v0

--- a/solution.py
+++ b/solution.py
@@ -15,7 +15,8 @@
     values_here = heads_here // GROUP
     change_rows = delta_v.reshape(delta_v.shape[0] // BLK, BLK * values_here * HD)
     flat_lists = key_lists.reshape(blocks_here * topk_here)
-    every_change = lax.all_gather(change_rows, "seq", axis=0, tiled=True)
+    copies = jnp.concatenate([change_rows] * lax.axis_size("seq"), axis=0)
+    every_change = lax.all_to_all(copies, "seq", 0, 0, tiled=True)
     onehot = (flat_lists[:, None] == changed_block_numbers[None, :]).astype(jnp.bfloat16)
     selected = jnp.dot(onehot, every_change, preferred_element_type=jnp.float32)
     picked = selected.astype(jnp.bfloat16).reshape(blocks_here, topk_here, BLK, values_here, HD)

time: 248 us -> 179 us (0.72)
  waiting for transfers between devices: 196 us -> 102 us
  starting transfers between devices: 0.12 us -> 11.9 us
  other arithmetic: 0.25 us -> 8.39 us
  local copies, waits for them, and re-layouts: 22.4 us -> 27.7 us
    all_gather x1 -> x0, waiting for transfers between devices: 72.4 us -> none  [local(): every_change = lax.all_gather(change_rows, 'seq', axis=0, tiled=True)]
    all_gather x1, waiting for transfers between devices: 83 us -> 39.7 us  [local(): lax.all_gather(w_out, 'seq', axis=1, tiled=True)]
    all_to_all x0 -> x1, waiting for transfers between devices: none -> 21.9 us  [local(): every_change = lax.all_to_all(copies, 'seq', 0, 0, tiled=True)]
    all_to_all x0 -> x1, starting transfers between devices: none -> 11.6 us  [local(): every_change = lax.all_to_all(copies, 'seq', 0, 0, tiled=True)]
    concatenate x0 -> x1, other arithmetic: none -> 7.05 us  [local(): copies = jnp.concatenate([change_rows] * lax.axis_size('seq'), axis=0)]
    concatenate x0 -> x2, local copies, waits for them, and re-layouts: none -> 3.15 us  [local(): copies = jnp.concatenate([change_rows] * lax.axis_size('seq'), axis=0)]
    unnamed x12 -> x13, local copies, waits for them, and re-layouts: 21.5 us -> 23.6 us
    unnamed x4 -> x3, waiting for transfers between devices: 40.7 us -> 40.7 us
  transfers between devices with their start and end apart: 3 -> 3, of which waited for: 3 -> 3; matrix products, arithmetic and copies ran while one was open for 7% -> 17% of each run, Pallas kernels for 0% -> 0%
where the time goes in v1:
time: 179 us; the launch traced here: 178 us
  waiting for transfers between devices  102 us (57%)
  local copies, waits for them, and re-layouts  27.7 us (15%)
  between operations  14.1 us (8%)
  matrix products  13.6 us (8%)
  starting transfers between devices  11.9 us (7%)
  other arithmetic  8.39 us (5%)
    unnamed x3, waiting for transfers between devices  40.7 us
    all_gather x1, waiting for transfers between devices, local(): lax.all_gather(w_out, 'seq', axis=1, tiled=True)  39.7 us
    unnamed x13, local copies, waits for them, and re-layouts  23.6 us
    all_to_all x1, waiting for transfers between devices, local(): every_change = lax.all_to_all(copies, 'seq', 0, 0, tiled=True)  21.9 us
    all_to_all x1, starting transfers between devices, local(): every_change = lax.all_to_all(copies, 'seq', 0, 0, tiled=True)  11.6 us
    dot_general x1, matrix products, local(): jnp.dot(attn_new, lax.all_gather(w_out, 'seq', axis=1, tiled=True), prefe...  8.93 us
    concatenate x1, other arithmetic, local(): copies = jnp.concatenate([change_rows] * lax.axis_size('seq'), axis=0)  7.05 us
    dot_general x1, matrix products, local(): jnp.einsum('qvgkij,qkjvd->qivgd', tiles, picked, preferred_element_type=j...  4.69 us
  transfers between devices with their start and end apart: 3, of which 3 were waited for; matrix products, arithmetic and copies ran while one was open for 17% of the time, Pallas kernels for 0%

profile of v1, /device:TPU:2, one launch (start us, length us, event | category | flops | bytes accessed | tf_op | source)
XLA Modules:
  0.0 177.9 jit_solution(17733729967381737898)
XLA Ops:
  7.2 0.0 all-gather.2.cloned.1.call-start
  7.2 0.7 all-gather.2.cloned.1.call-update
  7.9 2.6 %concatenate.6 = bf16[32,1,16384]{2,1,0:T(2,128)(2,1)S(1)} broadcast(bf16[16384]{0:T(1024)(128)(2,1)} %bitcast.36), dimensions={2} | broadcast | bytes 1081344 | tf_op jit(solution)/shard_map/concatenate | solution.py:18
  10.5 0.5 broadcast.5
  11.1 7.1 %reduce = bf16[32,16384]{1,0:T(8,128)(2,1)S(1)} reduce(bf16[32,1,16384]{2,1,0:T(2,128)(2,1)S(1)} %concatenate.6, bf16[]{:T(256)} %broadcast.5), dimensions={1}, to_apply=%concatenate.6.reduce_sub_computation | reduce | bytes 2097154 | tf_op jit(solution)/shard_map/concatenate | solution.py:18
  18.1 1.6 reshape.34
  19.7 11.6 %all-to-all-start = ((bf16[32,2,8192]{2,1,0:T(2,128)(2,1)}), bf16[32,2,8192]{2,1,0:T(2,128)(2,1)S(1)}, u32[]{:S(2)}, u32[]{:S(2)}) async-start(bf16[32,2,8192]{2,1,0:T(2,128)(2,1)} %reshape.34), calls=%async_computation | async-start | bytes 2097152 | tf_op jit(solution)/shard_map/all_to_all | solution.py:19
  31.4 0.0 copy-start.1
  31.4 0.0 copy-start
  31.4 0.0 copy-start.2
  31.4 0.2 reduce-scatter.4.cloned.1.call-start
  31.6 8.7 %copy.14 = bf16[4,5,8,128,128]{3,2,4,1,0:T(8,128)(2,1)} copy(bf16[4,5,8,128,128]{4,3,2,1,0:T(8,128)(2,1)} %param.6) | data formatting | bytes 10485760 | tf_op args[0]
  40.3 0.0 copy-done.1
  40.3 0.1 eq.15
  40.4 0.0 copy-done
  40.4 1.1 copy.13
  41.5 21.9 %all-to-all-done = bf16[32,2,8192]{2,1,0:T(2,128)(2,1)S(1)} async-done(((bf16[32,2,8192]{2,1,0:T(2,128)(2,1)}), bf16[32,2,8192]{2,1,0:T(2,128)(2,1)S(1)}, u32[]{:S(2)}, u32[]{:S(2)}) %all-to-all-start) | async-done | bytes 1048608 | tf_op jit(solution)/shard_map/all_to_all | solution.py:19
  63.3 1.0 reshape.35
  64.4 0.0 copy-done.2
  64.4 4.7 %convolution_bitcast_fusion = f32[4,128,1,5,128]{1,4,3,0,2:T(8,128)S(1)} fusion(bf16[4,5,8,128,128]{3,2,4,1,0:T(8,128)(2,1)} %copy.14, bf16[32,1,16384]{2,1,0:T(2,128)(2,1)S(1)} %reshape.35, s32[32]{0:T(128)S(1)} %copy-done.2, s32[32]{0:T(128)S(1)} %eq.15), kind=kOutput, calls=%fused_computation.2 | convolution fusion | flops 705168384 | bytes 7602432 | tf_op jit(solution)/shard_map/qvgkij,qkjvd->qivgd/dot_general | solution.py:24
  69.1 0.8 copy.15
  69.9 1.3 fusion.1
  71.3 39.7 %all-gather.2.cloned.1.call-done = bf16[640,5120]{0,1:T(8,128)(2,1)} async-done(((bf16[640,160]{0,1:T(8,128)(2,1)}), bf16[640,5120]{0,1:T(8,128)(2,1)}) %all-gather.2.cloned.1.call-update) | async-done | bytes 6553616 | tf_op jit(solution)/shard_map/all_gather | solution.py:29
  111.0 8.9 %convolution_convert_fusion.1 = bf16[512,5120]{1,0:T(8,128)(2,1)} fusion(bf16[512,640]{0,1:T(8,128)(2,1)S(1)} %fusion.1, bf16[640,5120]{0,1:T(8,128)(2,1)} %all-gather.2.cloned.1.call-done), kind=kOutput, calls=%fused_computation.1 | convolution fusion | flops 3358064640 | bytes 12451840 | tf_op jit(solution)/shard_map/dot_general | solution.py:27
  119.9 7.9 %copy.19 = bf16[512,5120]{0,1:T(8,128)(2,1)} copy(bf16[512,5120]{1,0:T(8,128)(2,1)} %convolution_convert_fusion.1) | data formatting | bytes 10485760
  127.9 0.0 reduce-scatter.4.cloned.1.call-update
  127.9 1.1 copy.16
  129.0 40.0 %reduce-scatter.4.cloned.1.call-done = bf16[640,512]{1,0:T(8,128)(2,1)} async-done(((bf16[5120,512]{1,0:T(8,128)(2,1)}), bf16[640,512]{1,0:T(8,128)(2,1)}) %reduce-scatter.4.cloned.1.call-update) | async-done | bytes 655376
  168.9 2.2 %copy.20 = bf16[512,640]{1,0:T(8,128)(2,1)} copy(bf16[512,640]{0,1:T(8,128)(2,1)} %bitcast.35) | data formatting | bytes 1310720
Async XLA Ops:
  7.2 103.8 %all-gather.2.cloned.1.call-start = ((), (), s32[]{:S(2)}) async-start(), calls=%async_computation.2 | async-start | bytes 6758400 | tf_op jit(solution)/shard_map/all_gather | solution.py:29
  19.7 43.6 %all-to-all-start = ((bf16[32,2,8192]{2,1,0:T(2,128)(2,1)}), bf16[32,2,8192]{2,1,0:T(2,128)(2,1)S(1)}, u32[]{:S(2)}, u32[]{:S(2)}) async-start(bf16[32,2,8192]{2,1,0:T(2,128)(2,1)} %reshape.34), calls=%async_computation | async-start | bytes 2097152 | tf_op jit(solution)/shard_map/all_to_all | solution.py:19
  31.4 8.9 %copy-start.1 = (s32[4,8]{1,0:T(4,128)S(1)}, s32[4,8]{1,0:T(4,128)}, u32[]{:S(2)}) copy-start(s32[4,8]{1,0:T(4,128)} %param.8) | copy-start | bytes 388
  31.4 9.0 %copy-start = (bf16[512,640]{1,0:T(8,128)(2,1)S(1)}, bf16[512,640]{1,0:T(8,128)(2,1)}, u32[]{:S(2)}) copy-start(bf16[512,640]{1,0:T(8,128)(2,1)} %param.7) | copy-start | bytes 1966084
  31.4 33.0 %copy-start.2 = (s32[32]{0:T(128)S(1)}, s32[32]{0:T(128)}, u32[]{:S(2)}) copy-start(s32[32]{0:T(128)} %param.9) | copy-start | bytes 388
  31.4 137.5 %reduce-scatter.4.cloned.1.call-start = ((), (), s32[]{:S(2)}) async-start(), calls=%async_computation.3 | async-start | bytes 5898240
Sparse Core Ops, SparseCore 0:
  10.6 100.3 all-gather.1
  128.0 40.8 reduce-scatter.3
